TPU v7x, 256 devices: a whole 4x4x8 slice. The times are simulated.
256 devices in a mesh: seq: 64 (over z_lo, x, y), tp: 4 (over z_hi, core).
Axes of the slice: x: 4, y: 4, z: 8 (z_hi: 2, z_lo: 4; z = z_hi * 4 + z_lo), core: 2. Of those that a mesh axis runs over, the one named last changes fastest.
Arguments:
- byte_states: bfloat16 [16384, 1024], P('seq'), may hold values from -6 to 6
- enc_gain: bfloat16 [1024], replicated, may hold values from 0.25 to 1.75
- enc_qkv: bfloat16 [3, 1024, 1024], P(None, None, 'tp')
- enc_proj_out: bfloat16 [1024, 1024], P('tp'), may hold values from -0.1875 to 0.1875
- starts: int32 [64, 64], P('seq'), may hold values from 0 to 16384, as said below
- counts: int32 [64], P('seq'), may hold values from 32 to 64, as said below
- lift: bfloat16 [1024, 4096], P(None, 'tp')
- cross_kv: bfloat16 [2, 1024, 4096], P(None, None, 'tp')
- latent_gain: bfloat16 [4096], replicated, may hold values from 0.25 to 1.75
- lat_qkv: bfloat16 [3, 4096, 2048], P(None, 'seq', 'tp')
- lat_proj_out: bfloat16 [2048, 4096], P('tp', 'seq'), may hold values from -0.75 to 0.75
Outputs:
- byte_out: bfloat16 [16384, 1024], P('seq')
- latent_out: bfloat16 [4096, 4096], P('seq', 'tp')
Inputs may be any that keep to these rules, and one draw needn't show every extreme that they name: `starts`: row s lists in increasing order the first byte (counted over all 16384 bytes) of each patch beginning in bytes s * 256 to (s + 1) * 256 - 1, then 16384 in unused places. Byte 0 begins a patch; every row's first patch begins fewer than 8 bytes into its block, and in some row exactly 7 bytes in. counts[s] is the number of patches listed in row s of starts; some row holds 64.
All inputs are finite; a program needn't handle non-finite values.
Results may differ from a plain program's by a relative error of at most 0.018.
Values may be sent and summed in bfloat16 or wider, within the bound.
No kernel may reach another device: no remote copies, remote signals or barrier semaphores. Data moves between devices by JAX's collectives and lax.ppermute only.
A program may use at most 128 MiB of HBM per device.

v0:
```python
import math
import jax
import jax.numpy as jnp
from jax import lax
from jax.sharding import Mesh
from jax.sharding import PartitionSpec as P

EH = 64
HD = 128
WIN = 512
SPILL = 8
SEQ = ("seq_0", "seq_1", "seq_2")
epsilon = 1e-05
rope_base = 500000.0
far_position = 1 << 30


def from_behind(value, axis, steps):
    count = lax.axis_size(axis)
    leading, last = (max(0, -steps), min(count, count - steps))
    return lax.ppermute(value, axis, [(source, source + steps) for source in range(leading, last)])


def from_everyone(value, axis):
    copies = jnp.broadcast_to(value, (lax.axis_size(axis), *value.shape))
    return lax.all_to_all(copies, axis, split_axis=0, concat_axis=0, tiled=True)


def taken_together(value, axis):
    everything = from_everyone(value, axis)
    return jnp.sum(everything, axis=0)


def combined_pairwise(pieces, combine):
    while len(jax.tree.leaves(pieces)[0]) > 1:
        pieces = jax.vmap(combine)(*(pieces[side::2] for side in (0, 1)))
    return pieces[0]


def carried_in(value, axis, combine, identity):
    length, index = (lax.axis_size(axis), lax.axis_index(axis))
    passed = jnp.arange(length) < index

    def kept(part, zero, own):
        part = jnp.where(
            passed.reshape(-1, *(1 for _ in own.shape)), part, jnp.asarray(zero, own.dtype)
        )
        return part

    pieces = from_everyone(value, axis)
    return combined_pairwise(kept(pieces, identity, value), combine)


def laid_out(tiles, dim):
    tiles = jnp.moveaxis(tiles, 0, dim)
    lengths = tiles.shape
    return tiles.reshape(*lengths[:dim], lengths[dim] * lengths[dim + 1], *lengths[dim + 2 :])


def gather_directly(value, axis, dim):
    tiles = from_everyone(value, axis)
    return laid_out(tiles, dim)


def edges_of(length, count):
    unit = 8 if length >= 8 * count else 1
    return [length // unit * k // count * unit for k in range(1, count)]


def gather_in_order(value, axes, turns):
    tiles = value
    for k in turns:
        tiles = lax.all_gather(tiles, axes[k])
    done = turns[::-1]
    back = [done.index(k) for k in range(len(axes))]
    tiles = tiles.transpose(*back, *range(len(axes), tiles.ndim))
    return tiles.reshape(-1, *value.shape)


def spread_gather(value, axes, dim):
    cut = max(range(max(1, value.ndim - 1)), key=lambda d: value.shape[d])
    count, done = (len(axes), [])
    for leading, slab in enumerate(jnp.split(value, edges_of(value.shape[cut], count), axis=cut)):
        if slab.size:
            turns = [(leading - k) % count for k in range(count)]
            done.append(gather_in_order(slab, axes, turns))
    return laid_out(jnp.concatenate(done, axis=cut + 1), dim)


def sent_together(arrays, axis, dim, along):
    ends, at = ([], 0)
    for a in arrays[:-1]:
        at += a.shape[along]
        ends.append(at)
    both = jnp.concatenate(arrays, axis=along)
    return tuple(jnp.split(lax.all_gather(both, axis, axis=dim, tiled=True), ends, axis=along))


def shortened(value):

    def short(part):
        return part.astype(jnp.bfloat16) if part.dtype == jnp.float32 else part

    return jax.tree.map(short, value)


def in_blocks(value, dim, length):
    before, after = (value.shape[:dim], value.shape[dim + 1 :])
    return jnp.moveaxis(value.reshape(*before, length, -1, *after), dim, 0)


def sum_at_owner(value, axis, dim):
    length = lax.axis_size(axis)
    tiles = lax.all_to_all(in_blocks(value, dim, length), axis, 0, 0, tiled=True)
    return jnp.sum(tiles, axis=0)


def rms_scale(values, gain_row):
    mean_square = jnp.mean(values * values, axis=-1, keepdims=True)
    return values * lax.rsqrt(mean_square + epsilon) * gain_row


def masked_softmax(scores, allowed):
    scores = jnp.where(allowed, scores, -1e30)
    largest = jnp.max(scores, axis=-1, keepdims=True)
    raised = jnp.where(allowed, jnp.exp(scores - largest), 0.0)
    return raised / jnp.sum(raised, axis=-1, keepdims=True)


def rotate(values, position):
    halfway = values.shape[-1] // 2
    frequency = jnp.power(
        rope_base, -2.0 * jnp.arange(halfway, dtype=jnp.float32) / values.shape[-1]
    )
    angles = position.astype(jnp.float32)[:, None] * frequency[None, :]
    cosine = jnp.cos(angles)[:, None, :]
    sine_rows = jnp.sin(angles)[:, None, :]
    lower_half = values[..., :halfway]
    upper_half = values[..., halfway:]
    return jnp.concatenate(
        [
            lower_half * cosine - upper_half * sine_rows,
            upper_half * cosine + lower_half * sine_rows,
        ],
        axis=-1,
    )


def patch_block(extended, first_byte, end_byte, in_use, anchor, lift, cross_kv):
    columns = anchor + jnp.arange(extended.shape[0], dtype=jnp.int32)
    inside = (
        (columns[None, :] >= first_byte[:, None])
        & (columns[None, :] < end_byte[:, None])
        & in_use[:, None]
    )
    member = inside.astype(jnp.bfloat16)
    totals = jnp.dot(member, extended, preferred_element_type=jnp.float32)
    lengths = jnp.maximum(jnp.sum(inside.astype(jnp.float32), axis=1), 1.0)
    pooled = (totals / lengths[:, None]).astype(jnp.bfloat16)
    lifted = jnp.dot(pooled, lift, preferred_element_type=jnp.float32)
    key_rows = jnp.dot(extended, cross_kv[0], preferred_element_type=jnp.float32).astype(
        jnp.bfloat16
    )
    value_rows = jnp.dot(extended, cross_kv[1], preferred_element_type=jnp.float32).astype(
        jnp.bfloat16
    )
    slot_total = first_byte.shape[0]
    head_count = lifted.shape[1] // HD
    queries = lifted.astype(jnp.bfloat16).reshape(slot_total, head_count, HD)
    scores = jnp.einsum(
        "phd,khd->hpk",
        queries,
        key_rows.reshape(-1, head_count, HD),
        preferred_element_type=jnp.float32,
    ) * (1.0 / math.sqrt(HD))
    allowed = inside | (~in_use)[:, None] & (columns[None, :] == anchor)
    weights = masked_softmax(scores, allowed[None]).astype(jnp.bfloat16)
    crossed = jnp.einsum(
        "hpk,khd->phd",
        weights,
        value_rows.reshape(-1, head_count, HD),
        preferred_element_type=jnp.float32,
    )
    crossed = crossed.reshape(slot_total, head_count * HD)
    return jnp.where(in_use[:, None], lifted + crossed, 0.0).astype(jnp.bfloat16)


def add_counts(earlier, later):
    return earlier + later


def shards(
    byte_states,
    enc_gain,
    enc_qkv,
    enc_proj_out,
    starts,
    counts,
    lift,
    cross_kv,
    latent_gain,
    lat_qkv,
    lat_proj_out,
):
    byte_rows = byte_states.shape[0]
    anchor = lax.axis_index(SEQ) * byte_rows
    states = byte_states.astype(jnp.float32)
    normed = rms_scale(states, enc_gain.astype(jnp.float32)).astype(jnp.bfloat16)
    projected = jnp.einsum(
        "bd,idc->ibc", normed, enc_qkv, preferred_element_type=jnp.float32
    ).astype(jnp.bfloat16)
    reach_blocks = max(WIN // byte_rows, 1)
    tail_rows = min(WIN, byte_rows)
    key_parts = []
    value_parts = []
    for distance in range(reach_blocks, 0, -1):
        moved_keys, moved_values = from_behind(
            (projected[1, byte_rows - tail_rows :], projected[2, byte_rows - tail_rows :]),
            SEQ,
            distance,
        )
        key_parts.append(moved_keys)
        value_parts.append(moved_values)
    key_rows = jnp.concatenate(key_parts + [projected[1]], axis=0)
    value_rows = jnp.concatenate(value_parts + [projected[2]], axis=0)
    head_count = projected.shape[2] // EH
    scores = jnp.einsum(
        "qhd,khd->hqk",
        projected[0].reshape(byte_rows, head_count, EH),
        key_rows.reshape(-1, head_count, EH),
        preferred_element_type=jnp.float32,
    ) * (1.0 / math.sqrt(EH))
    query_pos = anchor + jnp.arange(byte_rows, dtype=jnp.int32)
    key_pos = anchor - WIN + jnp.arange(WIN + byte_rows, dtype=jnp.int32)
    allowed = (
        (key_pos[None, :] <= query_pos[:, None])
        & (key_pos[None, :] > query_pos[:, None] - WIN)
        & (key_pos[None, :] >= 0)
    )
    weights = masked_softmax(scores, allowed[None]).astype(jnp.bfloat16)
    attended = jnp.einsum(
        "hqk,khd->qhd",
        weights,
        value_rows.reshape(-1, head_count, EH),
        preferred_element_type=jnp.float32,
    )
    attended = attended.reshape(byte_rows, head_count * EH).astype(jnp.bfloat16)
    blended = taken_together(
        jnp.dot(attended, enc_proj_out, preferred_element_type=jnp.float32), "tp"
    )
    encoded = (states + blended).astype(jnp.bfloat16)
    patch_count = counts[0]
    local_starts = starts[0]
    first_local = (local_starts[0:1] - anchor).astype(jnp.bfloat16)
    next_rows, next_first = from_behind((encoded[:SPILL], first_local), SEQ, -1)
    next_first = next_first.astype(jnp.int32)[0]
    extended = jnp.concatenate([encoded, next_rows], axis=0)
    slot_ids = jnp.arange(local_starts.shape[0], dtype=jnp.int32)
    in_use = slot_ids < patch_count
    following = jnp.concatenate([local_starts[1:], jnp.zeros((1,), jnp.int32)])
    patch_end = jnp.where(slot_ids + 1 < patch_count, following, anchor + byte_rows + next_first)
    patches = patch_block(extended, local_starts, patch_end, in_use, anchor, lift, cross_kv)
    offset = carried_in(counts, SEQ, add_counts, jnp.zeros((1,), jnp.int32))[0]
    position = offset + slot_ids
    slot_total = patches.shape[0]
    full_rows = gather_directly(patches, "tp", 1)
    normed_rows = rms_scale(full_rows.astype(jnp.float32), latent_gain.astype(jnp.float32)).astype(
        jnp.bfloat16
    )
    inner_width = lat_qkv.shape[2]
    projected = jnp.einsum(
        "pd,idc->ipc",
        normed_rows,
        spread_gather(lat_qkv, SEQ, 1),
        preferred_element_type=jnp.float32,
    )
    heads_here = inner_width // HD
    queries = rotate(projected[0].reshape(slot_total, heads_here, HD), position).astype(
        jnp.bfloat16
    )
    latent_keys = (
        rotate(projected[1].reshape(slot_total, heads_here, HD), position)
        .astype(jnp.bfloat16)
        .reshape(slot_total, inner_width)
    )
    latent_values = projected[2].astype(jnp.bfloat16)
    latent_pos = jnp.where(in_use, position, far_position)
    largest = jnp.full((heads_here, slot_total), -1e30, jnp.float32)
    piece_keys, piece_values, piece_pos = (
        *sent_together((latent_keys, latent_values), SEQ, 0, 1),
        lax.all_gather(shortened(latent_pos), SEQ, axis=0, tiled=True).astype(latent_pos.dtype),
    )
    rows_here = piece_keys.shape[0]
    piece_scores = jnp.einsum(
        "qhd,khd->hqk",
        queries,
        piece_keys.reshape(rows_here, heads_here, HD),
        preferred_element_type=jnp.float32,
    ) * (1.0 / math.sqrt(HD))
    permitted = (piece_pos[None, :] <= position[:, None])[None]
    piece_scores = jnp.where(permitted, piece_scores, -1e30)
    renewed = jnp.maximum(largest, jnp.max(piece_scores, axis=-1))
    raised = jnp.where(permitted, jnp.exp(piece_scores - renewed[..., None]), 0.0)
    weight_sum = jnp.sum(raised, axis=-1)
    weighted = jnp.einsum(
        "hqk,khd->hqd",
        raised.astype(jnp.bfloat16),
        piece_values.reshape(rows_here, heads_here, HD),
        preferred_element_type=jnp.float32,
    )
    largest, weight_sum, weighted = (renewed, weight_sum, weighted)
    latent_heads = (
        (weighted / weight_sum[..., None])
        .transpose(1, 0, 2)
        .reshape(slot_total, inner_width)
        .astype(jnp.bfloat16)
    )
    partials = jnp.dot(
        latent_heads,
        lax.all_gather(lat_proj_out, SEQ, axis=1, tiled=True),
        preferred_element_type=jnp.float32,
    )
    reduced = sum_at_owner(partials, "tp", 1)
    latent = jnp.where(in_use[:, None], patches.astype(jnp.float32) + reduced, 0.0).astype(
        jnp.bfloat16
    )
    return (encoded, latent)


def solution(mesh):
    finer = Mesh(mesh.devices.reshape(4, 4, 4, mesh.shape["tp"]), ("seq_0", "seq_1", "seq_2", "tp"))
    in_specs = (
        P(SEQ, None),
        P(),
        P(None, None, "tp"),
        P("tp", None),
        P(SEQ, None),
        P(SEQ),
        P(None, "tp"),
        P(None, None, "tp"),
        P(),
        P(None, SEQ, "tp"),
        P("tp", SEQ),
    )
    out_specs = (P(SEQ, None), P(SEQ, "tp"))
    return jax.shard_map(
        shards, mesh=finer, in_specs=in_specs, out_specs=out_specs, check_vma=False
    )
```

profile of v0, /device:TPU:1, one launch (start us, length us, event | category | flops | bytes accessed | tf_op | source)
XLA Modules:
  0.0 1065.7 jit_solution(14300211120696718170)
XLA Ops:
  7.2 1.1 fusion.121
  8.3 11.9 %all-gather.3 = bf16[12,24,512]{2,1,0:T(8,128)(2,1)} all-gather(bf16[3,24,512]{2,1,0:T(8,128)(2,1)S(1)} %get-tuple-element.15), channel_id=5, replica_groups=mesh['seq_0'=4,'seq_1'=4,'seq_2'=4,'tp'=4] {'seq_1'}, dimensions={0}, use_global_device_ids=true | all-gather | bytes 368640 | tf_op jit(solution)/shard_map/all_gather | solution.py:73
  20.4 10.7 %all-gather.6 = bf16[12,24,512]{2,1,0:T(8,128)(2,1)} all-gather(bf16[3,24,512]{2,1,0:T(8,128)(2,1)S(1)} %get-tuple-element.16), channel_id=8, replica_groups=mesh['seq_0'=4,'seq_1'=4,'seq_2'=4,'tp'=4] {'seq_2'}, dimensions={0}, use_global_device_ids=true | all-gather | bytes 368640 | tf_op jit(solution)/shard_map/all_gather | solution.py:73
  31.1 0.8 split.15
  31.9 13.9 %all-gather = bf16[12,16,512]{2,1,0:T(8,128)(2,1)S(1)} all-gather(bf16[3,16,512]{2,1,0:T(8,128)(2,1)S(1)} %split.15), channel_id=2, replica_groups=mesh['seq_0'=4,'seq_1'=4,'seq_2'=4,'tp'=4] {'seq_0'}, dimensions={0}, use_global_device_ids=true | all-gather | bytes 245760 | tf_op jit(solution)/shard_map/all_gather | solution.py:73
  45.8 12.3 %all-gather.1 = bf16[16,3,16,512]{3,2,1,0:T(8,128)(2,1)} all-gather(bf16[4,3,16,512]{3,2,1,0:T(8,128)(2,1)S(1)} %bitcast.170), channel_id=3, replica_groups=mesh['seq_0'=4,'seq_1'=4,'seq_2'=4,'tp'=4] {'seq_2'}, dimensions={0}, use_global_device_ids=true | all-gather | bytes 983040 | tf_op jit(solution)/shard_map/all_gather | solution.py:73
  58.2 5.4 all-gather.23.cloned.1.call-done
  63.9 2.2 fusion.41
  66.1 3.5 collective-permute-start.2
  69.6 3.2 collective-permute-start.3
  72.8 4.2 collective-permute-start
  77.0 2.5 collective-permute-start.1
  80.5 1.8 fusion.125
  83.7 2.5 broadcast_in_dim.134
  86.2 13.0 %all-to-all-start = ((f32[4,256,1024]{2,1,0:T(8,128)}), f32[4,256,1024]{2,1,0:T(8,128)}, u32[]{:S(2)}, u32[]{:S(2)}) async-start(f32[4,256,1024]{2,1,0:T(8,128)} %broadcast_in_dim.134), calls=%async_computation | async-start | bytes 8388608 | tf_op jit(solution)/shard_map/all_to_all | solution.py:26
  99.8 1.3 collective-permute-start.4
  101.9 2.7 collective-permute-done.4
  105.6 45.2 %all-to-all-done = f32[4,256,1024]{2,1,0:T(8,128)} async-done(((f32[4,256,1024]{2,1,0:T(8,128)}), f32[4,256,1024]{2,1,0:T(8,128)}, u32[]{:S(2)}, u32[]{:S(2)}) %all-to-all-start) | async-done | bytes 4194336 | tf_op jit(solution)/shard_map/all_to_all | solution.py:26
  151.4 59.0 %all-to-all-start.1 = ((s32[64,1,1]{2,1,0:T(1,128)}), s32[64,1,1]{2,1,0:T(1,128)S(1)}, u32[]{:S(2)}, u32[]{:S(2)}) async-start(s32[64,1,1]{2,1,0:T(1,128)} %broadcast_in_dim.141), calls=%async_computation.1 | async-start | bytes 65536 | tf_op jit(solution)/shard_map/all_to_all | solution.py:26
  210.4 3.2 reduce_sum.74
  213.6 1.2 fusion.66
  214.8 1.3 collective-permute-start.5
  216.1 3.6 collective-permute-done.5
  219.7 3.2 fusion.35
  222.9 1.8 fusion.44
  224.7 1.6 fusion.126
  226.3 2.3 fusion.38
  229.1 0.9 broadcast_in_dim.145
  229.9 5.0 all-to-all-start.2
  234.9 1.2 reduce.2
  239.3 4.0 copy.113
  243.2 11.5 %all-to-all-done.2 = bf16[4,64,1024]{2,1,0:T(8,128)(2,1)S(1)} async-done(((bf16[4,64,1024]{2,1,0:T(8,128)(2,1)}), bf16[4,64,1024]{2,1,0:T(8,128)(2,1)S(1)}, u32[]{:S(2)}, u32[]{:S(2)}) %all-to-all-start.2) | async-done | bytes 524320 | tf_op jit(solution)/shard_map/all_to_all | solution.py:26
  256.0 5.2 copy.114
  261.2 41.7 %all-gather.29.cloned.1.call-done = bf16[16,4,3,24,512]{4,3,2,1,0:T(8,128)(2,1)} async-done(((bf16[4,4,3,24,512]{4,3,2,1,0:T(8,128)(2,1)}), bf16[16,4,3,24,512]{4,3,2,1,0:T(8,128)(2,1)}) %all-gather.29.cloned.1.call-update) | async-done | bytes 4718608 | tf_op jit(solution)/shard_map/all_gather | solution.py:73
  302.9 6.3 maximum_bitcast_fusion
  309.2 1.8 copy.115
  311.0 2.2 convolution_bitcast_fusion.1
  314.6 0.7 all-gather.19.cloned.1.call-update
  316.8 316.5 %all-reduce = s32[4096]{0:T(1024)S(1)} all-reduce(s32[4096]{0:T(1024)S(1)} %select_dynamic-update-slice_fusion), channel_id=1, replica_groups=mesh['seq_0'=4,'seq_1'=4,'seq_2'=4,'tp'=4] {'seq_0','seq_1','seq_2'}, use_global_device_ids=true, to_apply=%add | all-reduce | flops 4096 | bytes 32768
  633.6 2.5 all-gather.17.cloned.1.call-done
  636.1 4.2 slice_bitcast_fusion.1
  640.3 1.8 fusion.131
  642.1 1.0 fusion.8
  643.2 1.1 fusion.55
  644.4 343.3 %all-gather.19.cloned.1.call-done = bf16[512,4096]{0,1:T(8,128)(2,1)} async-done(((bf16[512,64]{0,1:T(8,128)(2,1)}), bf16[512,4096]{0,1:T(8,128)(2,1)}) %all-gather.19.cloned.1.call-update) | async-done | bytes 4194320 | tf_op jit(solution)/shard_map/all_gather | solution.py:320
  987.7 3.7 convolution_bitcast_fusion
  991.4 66.6 %all_to_all.24 = f32[4,64,1024]{2,1,0:T(8,128)S(1)} all-to-all(f32[4,64,1024]{2,1,0:T(8,128)S(1)} %convolution_bitcast_fusion), channel_id=1, replica_groups=mesh['seq_0'=4,'seq_1'=4,'seq_2'=4,'tp'=4] {'tp'}, dimensions={0} | all-to-all | bytes 2097152 | tf_op jit(solution)/shard_map/all_to_all | solution.py:114
  1058.1 0.7 select_convert_fusion
  (109 shorter events, 10.4 us)
Async XLA Ops:
  7.2 215.7 %copy-start = (bf16[1024,1024]{1,0:T(8,128)(2,1)S(1)}, bf16[1024,1024]{1,0:T(8,128)(2,1)}, u32[]{:S(2)}) copy-start(bf16[1024,1024]{1,0:T(8,128)(2,1)} %param.17) | copy-start | bytes 6291460
  7.2 56.5 %copy-start.8 = (bf16[1024]{0:T(1024)(128)(2,1)S(1)}, bf16[1024]{0:T(1024)(128)(2,1)}, u32[]{:S(2)}) copy-start(bf16[1024]{0:T(1024)(128)(2,1)} %param.12) | copy-start | bytes 6148
  7.2 56.5 %copy-start.2 = (bf16[256,1024]{1,0:T(8,128)(2,1)S(1)}, bf16[256,1024]{1,0:T(8,128)(2,1)}, u32[]{:S(2)}) copy-start(bf16[256,1024]{1,0:T(8,128)(2,1)} %param.11) | copy-start | bytes 1572868
  7.2 56.4 %all-gather.23.cloned.1.call-start = ((), (), s32[]{:S(2)}) async-start(), calls=%async_computation.7 | async-start | bytes 1474560 | tf_op jit(solution)/shard_map/all_gather | solution.py:73
  20.3 78.8 %all-gather.27.cloned.1.call-start = ((), (), s32[]{:S(2)}) async-start(), calls=%async_computation.9 | async-start | bytes 1474560 | tf_op jit(solution)/shard_map/all_gather | solution.py:73
  31.1 208.2 %all-gather.21.cloned.1.call-start = ((), (), s32[]{:S(2)}) async-start(), calls=%async_computation.6 | async-start | bytes 3932160 | tf_op jit(solution)/shard_map/all_gather | solution.py:73
  58.1 197.9 %all-gather.25.cloned.1.call-start = ((), (), s32[]{:S(2)}) async-start(), calls=%async_computation.8 | async-start | bytes 5898240 | tf_op jit(solution)/shard_map/all_gather | solution.py:73
  66.1 13.7 %collective-permute-start.2 = (bf16[256,256]{0,1:T(8,128)(2,1)S(1)}, bf16[256,256]{0,1:T(8,128)(2,1)S(1)}, u32[]{:S(2)}, u32[]{:S(2)}) collective-permute-start(bf16[256,256]{0,1:T(8,128)(2,1)S(1)} %get-tuple-element.7), channel_id=1, source_target_pairs={{0,8},{4,12},{8,16},{12,20},{16,24},{20,28},{24,32},{28,36},{32,40... | collective-permute-start | bytes 393224 | tf_op jit(solution)/shard_map/ppermute | solution.py:21
  69.6 10.3 collective-permute-start.3
  72.8 9.5 collective-permute-start
  77.0 5.3 collective-permute-start.1
  82.3 1.0 copy-start.5
  86.2 13.5 %copy-start.7 = (s32[1,64]{1,0:T(1,128)S(1)}, s32[1,64]{1,0:T(1,128)}, u32[]{:S(2)}) copy-start(s32[1,64]{1,0:T(1,128)} %param.15) | copy-start | bytes 772
  86.2 15.5 %copy-start.6 = (bf16[4096]{0:T(1024)(128)(2,1)S(1)}, bf16[4096]{0:T(1024)(128)(2,1)}, u32[]{:S(2)}) copy-start(bf16[4096]{0:T(1024)(128)(2,1)} %param.19) | copy-start | bytes 24580
  86.2 64.6 %all-to-all-start = ((f32[4,256,1024]{2,1,0:T(8,128)}), f32[4,256,1024]{2,1,0:T(8,128)}, u32[]{:S(2)}, u32[]{:S(2)}) async-start(f32[4,256,1024]{2,1,0:T(8,128)} %broadcast_in_dim.134), calls=%async_computation | async-start | bytes 8388608 | tf_op jit(solution)/shard_map/all_to_all | solution.py:26
  99.1 203.8 %all-gather.29.cloned.1.call-start = ((), (), s32[]{:S(2)}) async-start(), calls=%async_computation.10 | async-start | bytes 5898240 | tf_op jit(solution)/shard_map/all_gather | solution.py:73
  99.8 4.8 collective-permute-start.4
  151.4 77.6 %all-to-all-start.1 = ((s32[64,1,1]{2,1,0:T(1,128)}), s32[64,1,1]{2,1,0:T(1,128)S(1)}, u32[]{:S(2)}, u32[]{:S(2)}) async-start(s32[64,1,1]{2,1,0:T(1,128)} %broadcast_in_dim.141), calls=%async_computation.1 | async-start | bytes 65536 | tf_op jit(solution)/shard_map/all_to_all | solution.py:26
  214.8 4.9 copy-start.3
  214.8 4.9 collective-permute-start.5
  222.9 3.4 copy-start.4
  229.9 24.8 %all-to-all-start.2 = ((bf16[4,64,1024]{2,1,0:T(8,128)(2,1)}), bf16[4,64,1024]{2,1,0:T(8,128)(2,1)S(1)}, u32[]{:S(2)}, u32[]{:S(2)}) async-start(bf16[4,64,1024]{2,1,0:T(8,128)(2,1)} %broadcast_in_dim.145), calls=%async_computation.2 | async-start | bytes 1048576 | tf_op jit(solution)/shard_map/all_to_all | solution.py:26
  234.9 401.2 %all-gather.17.cloned.1.call-start = ((), (), s32[]{:S(2)}) async-start(), calls=%async_computation.4 | async-start | bytes 8519680 | tf_op jit(solution)/shard_map/all_gather | solution.py:96
  311.0 4.3 copy-start.9
  314.5 673.1 %all-gather.19.cloned.1.call-start = ((), (), s32[]{:S(2)}) async-start(), calls=%async_computation.5 | async-start | bytes 4259840 | tf_op jit(solution)/shard_map/all_gather | solution.py:320
  987.7 71.2 %copy-start.1 = (bf16[1024,1024]{1,0:T(8,128)(2,1)S(1)}, bf16[1024,1024]{1,0:T(8,128)(2,1)}, u32[]{:S(2)}) copy-start(bf16[1024,1024]{1,0:T(8,128)(2,1)} %param.17) | copy-start | bytes 6291460
Sparse Core Ops, SparseCore 0:
  20.4 43.1 all-gather.22
  65.4 24.5 all-gather.26
  91.8 47.5 all-gather.20
  141.1 55.4 all-gather.24
  198.2 104.6 all-gather.28
  314.7 321.3 all-gather.16
  637.9 349.7 all-gather.18
where the time goes:
time: 1070 us
  waiting for transfers between devices  457 us (43%)
  blocking collectives  432 us (40%)
  starting transfers between devices  93.1 us (9%)
  local copies, waits for them, and re-layouts  25.2 us (2%)
  matrix products  22 us (2%)
  other arithmetic  18.3 us (2%)
  between operations  17.9 us (2%)
    all_gather x1, waiting for transfers between devices, shards(): lax.all_gather(lat_proj_out, SEQ, axis=1, tiled=True)  343 us
    unnamed x1, blocking collectives  317 us
    all_to_all x3, starting transfers between devices, from_everyone(): return lax.all_to_all(copies, axis, split_axis=0, concat_axis=0, tiled=True)  76.9 us
    all_to_all x1, blocking collectives, sum_at_owner(): lax.all_to_all(in_blocks(value, dim, length), axis, 0, 0, tiled=True)  66.6 us
    all_to_all x3, waiting for transfers between devices, from_everyone(): return lax.all_to_all(copies, axis, split_axis=0, concat_axis=0, tiled=True)  56.7 us
    all_gather x4, blocking collectives, gather_in_order(): tiles = lax.all_gather(tiles, axes[k])  48.8 us
    all_gather x5, waiting for transfers between devices, gather_in_order(): tiles = lax.all_gather(tiles, axes[k])  47.2 us
  transfers between devices with their start and end apart: 16, of which 8 were waited for; matrix products, arithmetic and copies ran while one was open for 5% of the time, Pallas kernels for 0%

commit v1 on v0

--- a/solution.py
+++ b/solution.py
@@ -13,6 +13,14 @@
 epsilon = 1e-05
 rope_base = 500000.0
 far_position = 1 << 30
+
+
+def extend_rails(vector, across, dim_k=1):
+    found_now = jnp.concatenate(
+        lax.all_to_all(jnp.stack([vector for _ in range(lax.axis_size(across))], 0), across, 0, 0),
+        dim_k,
+    )
+    return found_now
 
 
 def from_behind(value, axis, steps):
@@ -316,9 +324,7 @@
         .astype(jnp.bfloat16)
     )
     partials = jnp.dot(
-        latent_heads,
-        lax.all_gather(lat_proj_out, SEQ, axis=1, tiled=True),
-        preferred_element_type=jnp.float32,
+        latent_heads, extend_rails(lat_proj_out, SEQ), preferred_element_type=jnp.float32
     )
     reduced = sum_at_owner(partials, "tp", 1)
     latent = jnp.where(in_use[:, None], patches.astype(jnp.float32) + reduced, 0.0).astype(

time: 1070 us -> 812 us (0.76)
  waiting for transfers between devices: 457 us -> 111 us
  blocking collectives: 432 us -> 512 us
    all_gather x1 -> x0, waiting for transfers between devices: 343 us -> none  [shards(): lax.all_gather(lat_proj_out, SEQ, axis=1, tiled=True)]
    unnamed x1, blocking collectives: 317 us -> 392 us
  transfers between devices with their start and end apart: 16 -> 16, of which waited for: 8 -> 6; matrix products, arithmetic and copies ran while one was open for 5% -> 6% of each run, Pallas kernels for 0% -> 0%
where the time goes in v1:
time: 812 us; the launch traced here: 811 us
  blocking collectives  512 us (63%)
  waiting for transfers between devices  111 us (14%)
  starting transfers between devices  102 us (13%)
  local copies, waits for them, and re-layouts  27.6 us (3%)
  matrix products  22 us (3%)
  other arithmetic  18.3 us (2%)
  between operations  17.9 us (2%)
    unnamed x1, blocking collectives  392 us
    all_to_all x3, starting transfers between devices, from_everyone(): return lax.all_to_all(copies, axis, split_axis=0, concat_axis=0, tiled=True)  76.9 us
    all_to_all x1, blocking collectives, sum_at_owner(): lax.all_to_all(in_blocks(value, dim, length), axis, 0, 0, tiled=True)  71.3 us
    all_to_all x3, waiting for transfers between devices, from_everyone(): return lax.all_to_all(copies, axis, split_axis=0, concat_axis=0, tiled=True)  56.7 us
    all_gather x4, blocking collectives, gather_in_order(): tiles = lax.all_gather(tiles, axes[k])  48.8 us
    all_gather x5, waiting for transfers between devices, gather_in_order(): tiles = lax.all_gather(tiles, axes[k])  47.2 us
  transfers between devices with their start and end apart: 16, of which 6 were waited for; matrix products, arithmetic and copies ran while one was open for 6% of the time, Pallas kernels for 0%

profile of v1, /device:TPU:1, one launch (start us, length us, event | category | flops | bytes accessed | tf_op | source)
XLA Modules:
  0.0 810.9 jit_solution(15502911659330395364)
XLA Ops:
  7.2 1.1 fusion.121
  8.3 11.9 %all-gather.3 = bf16[12,24,512]{2,1,0:T(8,128)(2,1)} all-gather(bf16[3,24,512]{2,1,0:T(8,128)(2,1)S(1)} %get-tuple-element.15), channel_id=5, replica_groups=mesh['seq_0'=4,'seq_1'=4,'seq_2'=4,'tp'=4] {'seq_1'}, dimensions={0}, use_global_device_ids=true | all-gather | bytes 368640 | tf_op jit(solution)/shard_map/all_gather | solution.py:81
  20.4 10.7 %all-gather.6 = bf16[12,24,512]{2,1,0:T(8,128)(2,1)} all-gather(bf16[3,24,512]{2,1,0:T(8,128)(2,1)S(1)} %get-tuple-element.16), channel_id=8, replica_groups=mesh['seq_0'=4,'seq_1'=4,'seq_2'=4,'tp'=4] {'seq_2'}, dimensions={0}, use_global_device_ids=true | all-gather | bytes 368640 | tf_op jit(solution)/shard_map/all_gather | solution.py:81
  31.1 0.8 split.15
  31.9 13.9 %all-gather = bf16[12,16,512]{2,1,0:T(8,128)(2,1)S(1)} all-gather(bf16[3,16,512]{2,1,0:T(8,128)(2,1)S(1)} %split.15), channel_id=2, replica_groups=mesh['seq_0'=4,'seq_1'=4,'seq_2'=4,'tp'=4] {'seq_0'}, dimensions={0}, use_global_device_ids=true | all-gather | bytes 245760 | tf_op jit(solution)/shard_map/all_gather | solution.py:81
  45.8 12.3 %all-gather.1 = bf16[16,3,16,512]{3,2,1,0:T(8,128)(2,1)} all-gather(bf16[4,3,16,512]{3,2,1,0:T(8,128)(2,1)S(1)} %bitcast.173), channel_id=3, replica_groups=mesh['seq_0'=4,'seq_1'=4,'seq_2'=4,'tp'=4] {'seq_2'}, dimensions={0}, use_global_device_ids=true | all-gather | bytes 983040 | tf_op jit(solution)/shard_map/all_gather | solution.py:81
  58.2 5.4 all-gather.20.cloned.1.call-done
  63.9 2.2 fusion.41
  66.1 3.5 collective-permute-start.2
  69.6 3.2 collective-permute-start.3
  72.8 4.2 collective-permute-start
  77.0 2.5 collective-permute-start.1
  80.5 1.8 fusion.125
  82.3 0.7 fusion.43
  83.7 2.5 broadcast_in_dim.134
  86.2 13.0 %all-to-all-start = ((f32[4,256,1024]{2,1,0:T(8,128)}), f32[4,256,1024]{2,1,0:T(8,128)}, u32[]{:S(2)}, u32[]{:S(2)}) async-start(f32[4,256,1024]{2,1,0:T(8,128)} %broadcast_in_dim.134), calls=%async_computation | async-start | bytes 8388608 | tf_op jit(solution)/shard_map/all_to_all | solution.py:34
  99.8 1.3 collective-permute-start.4
  101.9 2.7 collective-permute-done.4
  105.6 45.2 %all-to-all-done = f32[4,256,1024]{2,1,0:T(8,128)} async-done(((f32[4,256,1024]{2,1,0:T(8,128)}), f32[4,256,1024]{2,1,0:T(8,128)}, u32[]{:S(2)}, u32[]{:S(2)}) %all-to-all-start) | async-done | bytes 4194336 | tf_op jit(solution)/shard_map/all_to_all | solution.py:34
  151.4 59.0 %all-to-all-start.1 = ((s32[64,1,1]{2,1,0:T(1,128)}), s32[64,1,1]{2,1,0:T(1,128)S(1)}, u32[]{:S(2)}, u32[]{:S(2)}) async-start(s32[64,1,1]{2,1,0:T(1,128)} %broadcast_in_dim.141), calls=%async_computation.1 | async-start | bytes 65536 | tf_op jit(solution)/shard_map/all_to_all | solution.py:34
  210.4 3.2 reduce_sum.74
  213.6 1.2 fusion.66
  214.8 1.3 collective-permute-start.5
  216.1 3.6 collective-permute-done.5
  219.7 3.2 fusion.35
  222.9 1.8 fusion.44
  224.7 1.6 fusion.126
  226.3 2.3 fusion.38
  229.1 0.9 broadcast_in_dim.145
  229.9 5.0 all-to-all-start.2
  234.9 1.2 reduce.2
  239.3 4.0 copy.113
  243.2 11.5 %all-to-all-done.2 = bf16[4,64,1024]{2,1,0:T(8,128)(2,1)S(1)} async-done(((bf16[4,64,1024]{2,1,0:T(8,128)(2,1)}), bf16[4,64,1024]{2,1,0:T(8,128)(2,1)S(1)}, u32[]{:S(2)}, u32[]{:S(2)}) %all-to-all-start.2) | async-done | bytes 524320 | tf_op jit(solution)/shard_map/all_to_all | solution.py:34
  256.0 5.2 copy.114
  261.2 41.7 %all-gather.26.cloned.1.call-done = bf16[16,4,3,24,512]{4,3,2,1,0:T(8,128)(2,1)} async-done(((bf16[4,4,3,24,512]{4,3,2,1,0:T(8,128)(2,1)}), bf16[16,4,3,24,512]{4,3,2,1,0:T(8,128)(2,1)}) %all-gather.26.cloned.1.call-update) | async-done | bytes 4718608 | tf_op jit(solution)/shard_map/all_gather | solution.py:81
  302.9 6.3 maximum_bitcast_fusion
  309.2 1.8 copy.115
  311.0 2.2 convolution_bitcast_fusion.1
  314.6 2.4 stack.2
  317.0 9.1 %all-to-all-start.3 = ((bf16[64,512,64]{1,2,0:T(8,128)(2,1)}), bf16[64,512,64]{1,2,0:T(8,128)(2,1)}, u32[]{:S(2)}, u32[]{:S(2)}) async-start(bf16[64,512,64]{1,2,0:T(8,128)(2,1)} %stack.2), calls=%async_computation.3 | async-start | bytes 8388608 | tf_op jit(solution)/shard_map/all_to_all | solution.py:20
  327.6 392.1 %all-reduce = s32[4096]{0:T(1024)S(1)} all-reduce(s32[4096]{0:T(1024)S(1)} %select_dynamic-update-slice_fusion), channel_id=1, replica_groups=mesh['seq_0'=4,'seq_1'=4,'seq_2'=4,'tp'=4] {'seq_0','seq_1','seq_2'}, use_global_device_ids=true, to_apply=%add | all-reduce | flops 4096 | bytes 32768
  719.9 4.2 slice_bitcast_fusion.1
  724.1 1.8 fusion.131
  726.0 1.0 fusion.8
  727.0 1.1 fusion.55
  728.3 3.7 convolution_bitcast_fusion
  732.0 71.3 %all_to_all.29 = f32[4,64,1024]{2,1,0:T(8,128)S(1)} all-to-all(f32[4,64,1024]{2,1,0:T(8,128)S(1)} %convolution_bitcast_fusion), channel_id=1, replica_groups=mesh['seq_0'=4,'seq_1'=4,'seq_2'=4,'tp'=4] {'tp'}, dimensions={0} | all-to-all | bytes 2097152 | tf_op jit(solution)/shard_map/all_to_all | solution.py:122
  803.3 0.7 select_convert_fusion
  (111 shorter events, 9.7 us)
Async XLA Ops:
  7.2 215.7 %copy-start = (bf16[1024,1024]{1,0:T(8,128)(2,1)S(1)}, bf16[1024,1024]{1,0:T(8,128)(2,1)}, u32[]{:S(2)}) copy-start(bf16[1024,1024]{1,0:T(8,128)(2,1)} %param.17) | copy-start | bytes 6291460
  7.2 56.5 %copy-start.9 = (bf16[1024]{0:T(1024)(128)(2,1)S(1)}, bf16[1024]{0:T(1024)(128)(2,1)}, u32[]{:S(2)}) copy-start(bf16[1024]{0:T(1024)(128)(2,1)} %param.12) | copy-start | bytes 6148
  7.2 56.5 %copy-start.2 = (bf16[256,1024]{1,0:T(8,128)(2,1)S(1)}, bf16[256,1024]{1,0:T(8,128)(2,1)}, u32[]{:S(2)}) copy-start(bf16[256,1024]{1,0:T(8,128)(2,1)} %param.11) | copy-start | bytes 1572868
  7.2 56.4 %all-gather.20.cloned.1.call-start = ((), (), s32[]{:S(2)}) async-start(), calls=%async_computation.7 | async-start | bytes 1474560 | tf_op jit(solution)/shard_map/all_gather | solution.py:81
  20.3 78.8 %all-gather.24.cloned.1.call-start = ((), (), s32[]{:S(2)}) async-start(), calls=%async_computation.9 | async-start | bytes 1474560 | tf_op jit(solution)/shard_map/all_gather | solution.py:81
  31.1 208.2 %all-gather.18.cloned.1.call-start = ((), (), s32[]{:S(2)}) async-start(), calls=%async_computation.6 | async-start | bytes 3932160 | tf_op jit(solution)/shard_map/all_gather | solution.py:81
  58.1 197.9 %all-gather.22.cloned.1.call-start = ((), (), s32[]{:S(2)}) async-start(), calls=%async_computation.8 | async-start | bytes 5898240 | tf_op jit(solution)/shard_map/all_gather | solution.py:81
  66.1 13.7 %collective-permute-start.2 = (bf16[256,256]{0,1:T(8,128)(2,1)S(1)}, bf16[256,256]{0,1:T(8,128)(2,1)S(1)}, u32[]{:S(2)}, u32[]{:S(2)}) collective-permute-start(bf16[256,256]{0,1:T(8,128)(2,1)S(1)} %get-tuple-element.7), channel_id=1, source_target_pairs={{0,8},{4,12},{8,16},{12,20},{16,24},{20,28},{24,32},{28,36},{32,40... | collective-permute-start | bytes 393224 | tf_op jit(solution)/shard_map/ppermute | solution.py:29
  69.6 10.3 %collective-permute-start.3 = (bf16[256,256]{0,1:T(8,128)(2,1)S(1)}, bf16[256,256]{0,1:T(8,128)(2,1)S(1)}, u32[]{:S(2)}, u32[]{:S(2)}) collective-permute-start(bf16[256,256]{0,1:T(8,128)(2,1)S(1)} %get-tuple-element.7), channel_id=1, source_target_pairs={{0,4},{4,8},{8,12},{12,16},{16,20},{20,24},{24,28},{28,32},{32,36}... | collective-permute-start | bytes 393224 | tf_op jit(solution)/shard_map/ppermute | solution.py:29
  72.8 9.5 %collective-permute-start = (bf16[256,256]{0,1:T(8,128)(2,1)S(1)}, bf16[256,256]{0,1:T(8,128)(2,1)S(1)}, u32[]{:S(2)}, u32[]{:S(2)}) collective-permute-start(bf16[256,256]{0,1:T(8,128)(2,1)S(1)} %get-tuple-element.6), channel_id=1, source_target_pairs={{0,8},{4,12},{8,16},{12,20},{16,24},{20,28},{24,32},{28,36},{32,40... | collective-permute-start | bytes 393224 | tf_op jit(solution)/shard_map/ppermute | solution.py:29
  77.0 5.3 collective-permute-start.1
  82.3 1.0 copy-start.5
  86.2 13.5 %copy-start.8 = (s32[1,64]{1,0:T(1,128)S(1)}, s32[1,64]{1,0:T(1,128)}, u32[]{:S(2)}) copy-start(s32[1,64]{1,0:T(1,128)} %param.15) | copy-start | bytes 772
  86.2 15.5 %copy-start.7 = (bf16[4096]{0:T(1024)(128)(2,1)S(1)}, bf16[4096]{0:T(1024)(128)(2,1)}, u32[]{:S(2)}) copy-start(bf16[4096]{0:T(1024)(128)(2,1)} %param.19) | copy-start | bytes 24580
  86.2 64.6 %all-to-all-start = ((f32[4,256,1024]{2,1,0:T(8,128)}), f32[4,256,1024]{2,1,0:T(8,128)}, u32[]{:S(2)}, u32[]{:S(2)}) async-start(f32[4,256,1024]{2,1,0:T(8,128)} %broadcast_in_dim.134), calls=%async_computation | async-start | bytes 8388608 | tf_op jit(solution)/shard_map/all_to_all | solution.py:34
  99.1 203.8 %all-gather.26.cloned.1.call-start = ((), (), s32[]{:S(2)}) async-start(), calls=%async_computation.10 | async-start | bytes 5898240 | tf_op jit(solution)/shard_map/all_gather | solution.py:81
  99.8 4.8 collective-permute-start.4
  151.4 77.6 %all-to-all-start.1 = ((s32[64,1,1]{2,1,0:T(1,128)}), s32[64,1,1]{2,1,0:T(1,128)S(1)}, u32[]{:S(2)}, u32[]{:S(2)}) async-start(s32[64,1,1]{2,1,0:T(1,128)} %broadcast_in_dim.141), calls=%async_computation.1 | async-start | bytes 65536 | tf_op jit(solution)/shard_map/all_to_all | solution.py:34
  214.8 4.9 copy-start.3
  214.8 4.9 collective-permute-start.5
  222.9 3.4 copy-start.4
  229.9 24.8 %all-to-all-start.2 = ((bf16[4,64,1024]{2,1,0:T(8,128)(2,1)}), bf16[4,64,1024]{2,1,0:T(8,128)(2,1)S(1)}, u32[]{:S(2)}, u32[]{:S(2)}) async-start(bf16[4,64,1024]{2,1,0:T(8,128)(2,1)} %broadcast_in_dim.145), calls=%async_computation.2 | async-start | bytes 1048576 | tf_op jit(solution)/shard_map/all_to_all | solution.py:34
  234.9 485.0 %all-gather.16.cloned.1.call-start = ((), (), s32[]{:S(2)}) async-start(), calls=%async_computation.5 | async-start | bytes 8519680 | tf_op jit(solution)/shard_map/all_gather | solution.py:104
  311.0 3.6 copy-start.6
  317.0 9.1 %copy-start.10 = (u32[256]{0:T(256)S(1)}, u32[256]{0:T(256)}, u32[]{:S(2)}) copy-start(u32[256]{0:T(256)} %constant.69) | copy-start | bytes 3076
  317.0 411.2 %all-to-all-start.3 = ((bf16[64,512,64]{1,2,0:T(8,128)(2,1)}), bf16[64,512,64]{1,2,0:T(8,128)(2,1)}, u32[]{:S(2)}, u32[]{:S(2)}) async-start(bf16[64,512,64]{1,2,0:T(8,128)(2,1)} %stack.2), calls=%async_computation.3 | async-start | bytes 8388608 | tf_op jit(solution)/shard_map/all_to_all | solution.py:20
  728.2 75.8 %copy-start.1 = (bf16[1024,1024]{1,0:T(8,128)(2,1)S(1)}, bf16[1024,1024]{1,0:T(8,128)(2,1)}, u32[]{:S(2)}) copy-start(bf16[1024,1024]{1,0:T(8,128)(2,1)} %param.17) | copy-start | bytes 6291460
Sparse Core Ops, SparseCore 0:
  20.4 43.1 all-gather.19
  65.4 24.5 all-gather.23
  91.8 47.5 all-gather.17
  141.1 55.4 all-gather.21
  198.2 104.6 all-gather.25
  314.7 360.1 all-gather.15
